TPU v7x, 512 devices: a whole 4x8x8 slice. The times are simulated.
512 devices in a mesh: expert: 16 (over x, y_hi), tensor: 32 (over z, y_lo, core).
Axes of the slice: x: 4, y: 8 (y_hi: 4, y_lo: 2; y = y_hi * 2 + y_lo), z: 8, core: 2. Of those that a mesh axis runs over, the one named last changes fastest.
Arguments:
- tokens: bfloat16 [2048, 6144], P('expert'), may hold values from -6 to 6
- routes: int32 [2048, 4], P('expert'), may hold values from 0 to 15, all different within a row; in each aligned block of 128 rows (0 to 127, 128 to 255, ...) at most 40 rows name the same one
- gates: float32 [2048, 4], P('expert'), may hold values from 0.05 to 1
- gate_proj: bfloat16 [16, 2688, 6144], P('expert', 'tensor'), may hold values from -0.078125 to 0.078125
- up_proj: bfloat16 [16, 2688, 6144], P('expert', 'tensor'), may hold values from -0.078125 to 0.078125
- down_proj: bfloat16 [16, 6144, 2688], P('expert', 'tensor'), may hold values from -0.0625 to 0.0625
Outputs:
- combined: bfloat16 [2048, 6144], P('expert', 'tensor')
Inputs may be any that keep to these rules, and one draw needn't show every extreme that they name: `routes`: the ids of one row are distinct. In each aligned block of 128 rows no id is named by more than 40 rows, a bound that some block reaches.
All inputs are finite; a program needn't handle non-finite values.
Results may differ from a plain program's by a relative error of at most 0.0057.
Values may be sent and summed in bfloat16 or wider, within the bound.
No kernel may reach another device: no remote copies, remote signals or barrier semaphores. Data moves between devices by JAX's collectives and lax.ppermute only.
A program may use at most 64 MiB of HBM per device.

v0:
```python
import jax
import jax.numpy as jnp
from jax import lax
from jax.sharding import PartitionSpec as P

WIN = 4
CAP = 40


def slot_tables(route_block, gate_block):
    row_count = route_block.shape[0]
    experts = jnp.arange(WIN, dtype=jnp.int32)
    hits = route_block[None, :, :] == experts[:, None, None]
    chosen = jnp.any(hits, axis=2)
    position = jnp.cumsum(chosen.astype(jnp.int32), axis=1) - 1
    slots = jnp.arange(CAP, dtype=jnp.int32)
    match = chosen[:, None, :] & (position[:, None, :] == slots[None, :, None])
    row_ids = jnp.arange(row_count, dtype=jnp.int32)
    row_index = jnp.sum(jnp.where(match, row_ids[None, None, :], 0), axis=2)
    filled = jnp.any(match, axis=2)
    weight = jnp.sum(
        jnp.where(hits, gate_block[None, :, :], jnp.zeros((), gate_block.dtype)), axis=2
    )
    return (position, row_index, filled, weight)


def contract_last(left, right):
    return lax.dot_general(
        left, right, (((1,), (1,)), ((), ())), preferred_element_type=jnp.float32
    )


def body(tokens, routes, gates, gate_proj, up_proj, down_proj):
    groups = lax.axis_size("expert")
    split = groups // WIN
    width = tokens.shape[1]
    w_gate = gate_proj[0]
    w_up = up_proj[0]
    w_down = down_proj[0]
    position, row_index, filled, weight = slot_tables(routes, gates)
    picked = jnp.take(tokens, row_index, axis=0)
    picked = jnp.where(filled[:, :, None], picked, jnp.zeros((), tokens.dtype))
    outgoing = jnp.repeat(picked, split, axis=0)
    slot_rows = groups * CAP
    arrived = lax.all_to_all(outgoing, "expert", split_axis=0, concat_axis=0, tiled=True)
    flat_rows = arrived.reshape(slot_rows, width)
    gate_act = contract_last(flat_rows, w_gate)
    up_act = contract_last(flat_rows, w_up)
    hidden = (jax.nn.silu(gate_act) * up_act).astype(jnp.bfloat16)
    partial_value = contract_last(lax.all_gather(hidden, "tensor", axis=1, tiled=True), w_down)
    partial_value = partial_value.astype(jnp.bfloat16).reshape(groups, CAP, w_down.shape[0])
    returned = lax.all_to_all(partial_value, "expert", split_axis=0, concat_axis=0, tiled=True)
    expert_out = returned.astype(jnp.float32).reshape(WIN, split, CAP, w_down.shape[0]).sum(axis=1)
    flat_sum = expert_out.reshape(WIN * CAP, w_down.shape[0])
    offsets = jnp.arange(WIN, dtype=jnp.int32)[:, None] * CAP
    index = offsets + jnp.clip(position, 0, CAP - 1)
    values = jnp.take(flat_sum, index, axis=0)
    return jnp.sum(values * weight[:, :, None], axis=0).astype(jnp.bfloat16)


def solution(mesh):
    in_specs = (
        P("expert", None),
        P("expert", None),
        P("expert", None),
        P("expert", "tensor", None),
        P("expert", "tensor", None),
        P("expert", "tensor", None),
    )
    out_specs = P("expert", "tensor")
    return jax.shard_map(body, mesh=mesh, in_specs=in_specs, out_specs=out_specs, check_vma=False)
```

profile of v0, /device:TPU:8, one launch (start us, length us, event | category | flops | bytes accessed | tf_op | source)
XLA Modules:
  0.0 313.3 jit_solution(4435394938757956688)
XLA Ops:
  6.5 0.8 fusion.8
  7.4 0.3 reduce_window_sum.11
  7.7 0.1 select_reduce_fusion
  7.9 0.1 fusion.7
  8.0 0.1 reshape.122
  8.1 1.7 gather_fusion
  9.8 0.3 select_select_fusion
  10.1 1.0 broadcast_in_dim.76
  11.1 152.1 %all_to_all.10 = bf16[16,40,6144]{2,1,0:T(8,128)(2,1)S(1)} all-to-all(bf16[16,40,6144]{2,1,0:T(8,128)(2,1)S(1)} %bitcast.38), channel_id=1, replica_groups=mesh['expert'=16,'tensor'=32] {'expert'}, dimensions={0} | all-to-all | bytes 15728640 | tf_op jit(solution)/shard_map/all_to_all | solution.py:45
  163.3 2.5 fusion.3
  165.7 3.1 %fusion.1 = bf16[1,84,640]{2,1,0:T(8,128)(2,1)} fusion(bf16[640,6144]{1,0:T(8,128)(2,1)S(1)} %bitcast.37, bf16[1,84,6144]{2,1,0:T(8,128)(2,1)S(1)} %copy-done.4, f32[640,84]{0,1:T(8,128)S(1)} %fusion.3), kind=kOutput, calls=%fused_computation.6 | convolution fusion | flops 660925440 | bytes 9219072 | tf_op jit(solution)/shard_map/dot_general | solution.py:28
  168.9 0.0 all-gather.3.cloned.1.call-update
  168.9 101.5 %all-gather.3.cloned.1.call-done = bf16[32,84,640]{2,1,0:T(8,128)(2,1)} async-done(((bf16[1,84,640]{2,1,0:T(8,128)(2,1)}), bf16[32,84,640]{2,1,0:T(8,128)(2,1)}) %all-gather.3.cloned.1.call-update) | async-done | bytes 3440656 | tf_op jit(solution)/shard_map/all_gather | solution.py:50
  270.5 5.5 %reshape.139 = bf16[2688,640]{1,0:T(8,128)(2,1)} reshape(bf16[32,84,640]{2,1,0:T(8,128)(2,1)} %all-gather.3.cloned.1.call-done) | data formatting | bytes 6881280
  276.0 3.0 convolution_convert_fusion
  279.0 0.9 copy.18
  279.9 9.0 %all-to-all-start.1 = ((bf16[16,40,192]{2,1,0:T(8,128)(2,1)}), bf16[16,40,192]{2,1,0:T(8,128)(2,1)S(1)}, u32[]{:S(2)}, u32[]{:S(2)}) async-start(bf16[16,40,192]{2,1,0:T(8,128)(2,1)} %bitcast.9), calls=%async_computation.1 | async-start | bytes 655360 | tf_op jit(solution)/shard_map/all_to_all | solution.py:52
  288.8 0.1 fusion.9
  289.0 0.1 compare_and_fusion.1
  289.0 14.8 %all-to-all-done.1 = bf16[16,40,192]{2,1,0:T(8,128)(2,1)S(1)} async-done(((bf16[16,40,192]{2,1,0:T(8,128)(2,1)}), bf16[16,40,192]{2,1,0:T(8,128)(2,1)S(1)}, u32[]{:S(2)}, u32[]{:S(2)}) %all-to-all-start.1) | async-done | bytes 245792 | tf_op jit(solution)/shard_map/all_to_all | solution.py:52
  303.8 0.1 convert_reduce_fusion
  303.9 1.6 gather_fusion.1
  305.5 0.2 multiply_reduce_fusion
  305.7 0.7 copy.19
  (21 shorter events, 0.1 us)
Async XLA Ops:
  6.5 1.6 copy-start
  6.5 263.9 %all-gather.3.cloned.1.call-start = ((), (), s32[]{:S(2)}) async-start(), calls=%async_computation.2 | async-start | bytes 3717120 | tf_op jit(solution)/shard_map/all_gather | solution.py:50
  11.1 152.2 %copy-start.1 = (bf16[1,84,6144]{2,1,0:T(8,128)(2,1)S(1)}, bf16[1,84,6144]{2,1,0:T(8,128)(2,1)}, u32[]{:S(2)}) copy-start(bf16[1,84,6144]{2,1,0:T(8,128)(2,1)} %param.9) | copy-start | bytes 3096580
  163.3 2.5 copy-start.4
  168.9 107.1 %copy-start.5 = (bf16[1,192,2688]{2,1,0:T(8,128)(2,1)S(1)}, bf16[1,192,2688]{2,1,0:T(8,128)(2,1)}, u32[]{:S(2)}) copy-start(bf16[1,192,2688]{2,1,0:T(8,128)(2,1)} %param.11) | copy-start | bytes 3096580
  276.0 13.0 %copy-start.2 = (s32[128,4]{0,1:T(4,128)S(1)}, s32[128,4]{0,1:T(4,128)}, u32[]{:S(2)}) copy-start(s32[128,4]{0,1:T(4,128)} %param.7) | copy-start | bytes 6148
  276.0 13.0 %copy-start.3 = (f32[128,4]{0,1:T(4,128)S(1)}, f32[128,4]{0,1:T(4,128)}, u32[]{:S(2)}) copy-start(f32[128,4]{0,1:T(4,128)} %param.8) | copy-start | bytes 6148
  279.9 24.0 %all-to-all-start.1 = ((bf16[16,40,192]{2,1,0:T(8,128)(2,1)}), bf16[16,40,192]{2,1,0:T(8,128)(2,1)S(1)}, u32[]{:S(2)}, u32[]{:S(2)}) async-start(bf16[16,40,192]{2,1,0:T(8,128)(2,1)} %bitcast.9), calls=%async_computation.1 | async-start | bytes 655360 | tf_op jit(solution)/shard_map/all_to_all | solution.py:52
Sparse Core Ops, SparseCore 0:
  169.0 101.3 all-gather.2
where the time goes:
time: 314 us; the launch traced here: 313 us
  blocking collectives  152 us (48%)
  waiting for transfers between devices  116 us (37%)
  between operations  13.5 us (4%)
  local copies, waits for them, and re-layouts  11.5 us (4%)
  starting transfers between devices  8.98 us (3%)
  matrix products  8.59 us (3%)
    all_to_all x1, blocking collectives, body(): lax.all_to_all(outgoing, 'expert', split_axis=0, concat_axis=0, tiled=True)  152 us
    all_gather x1, waiting for transfers between devices, body(): lax.all_gather(hidden, 'tensor', axis=1, tiled=True)  102 us
    all_to_all x1, waiting for transfers between devices, body(): lax.all_to_all(partial_value, 'expert', split_axis=0, concat_axis=0, tile...  14.8 us
    all_to_all x1, starting transfers between devices, body(): lax.all_to_all(partial_value, 'expert', split_axis=0, concat_axis=0, tile...  8.98 us
    dot_general x3, matrix products, contract_last(): lax.dot_general(left, right, (((1,), (1,)), ((), ())), preferred_element_...  8.59 us
  transfers between devices with their start and end apart: 2, of which 2 were waited for; matrix products, arithmetic and copies ran while one was open for 0% of the time, Pallas kernels for 0%

commit v1 on v0

--- a/solution.py
+++ b/solution.py
@@ -5,6 +5,10 @@
 
 WIN = 4
 CAP = 40
+answer_boxes = lambda inner_x, chip_axis: jnp.concatenate(
+    lax.all_to_all(jnp.stack([inner_x for _ in range(lax.axis_size(chip_axis))]), chip_axis, 0, 0),
+    axis=1,
+)
 
 
 def slot_tables(route_block, gate_block):
@@ -47,7 +51,7 @@
     gate_act = contract_last(flat_rows, w_gate)
     up_act = contract_last(flat_rows, w_up)
     hidden = (jax.nn.silu(gate_act) * up_act).astype(jnp.bfloat16)
-    partial_value = contract_last(lax.all_gather(hidden, "tensor", axis=1, tiled=True), w_down)
+    partial_value = contract_last(answer_boxes(hidden, "tensor"), w_down)
     partial_value = partial_value.astype(jnp.bfloat16).reshape(groups, CAP, w_down.shape[0])
     returned = lax.all_to_all(partial_value, "expert", split_axis=0, concat_axis=0, tiled=True)
     expert_out = returned.astype(jnp.float32).reshape(WIN, split, CAP, w_down.shape[0]).sum(axis=1)

time: 314 us -> 332 us (1.057)
  the two profiles are of different devices: /device:TPU:8 before, /device:TPU:128 now
where the time goes in v1:
time: 332 us
  blocking collectives  186 us (56%)
  waiting for transfers between devices  109 us (33%)
  local copies, waits for them, and re-layouts  13.7 us (4%)
  starting transfers between devices  12.9 us (4%)
  matrix products  7.94 us (2%)
    all_to_all x1, blocking collectives, body(): lax.all_to_all(outgoing, 'expert', split_axis=0, concat_axis=0, tiled=True)  186 us
    all_to_all x1, waiting for transfers between devices, lax.all_to_all(jnp.stack([inner_x for _ in range(lax.axis_size(chip_axis)...  95.4 us
    all_to_all x1, waiting for transfers between devices, body(): lax.all_to_all(partial_value, 'expert', split_axis=0, concat_axis=0, tile...  13.6 us
    all_to_all x1, starting transfers between devices, lax.all_to_all(jnp.stack([inner_x for _ in range(lax.axis_size(chip_axis)...  9.26 us
    dot_general x3, matrix products, contract_last(): lax.dot_general(left, right, (((1,), (1,)), ((), ())), preferred_element_...  7.94 us
  transfers between devices with their start and end apart: 2, of which 2 were waited for; matrix products, arithmetic and copies ran while one was open for 0% of the time, Pallas kernels for 0%

profile of v1, /device:TPU:128, one launch (start us, length us, event | category | flops | bytes accessed | tf_op | source)
XLA Modules:
  0.0 331.8 jit_solution(326066754998085042)
XLA Ops:
  0.0 0.8 fusion.7
  0.8 0.3 reduce_window_sum.11
  1.1 0.1 select_reduce_fusion
  1.3 0.1 fusion.6
  1.5 0.1 reshape.132
  1.6 1.7 gather_fusion
  3.3 0.3 select_select_fusion
  3.6 1.0 broadcast_in_dim.76
  4.6 185.9 %all_to_all.15 = bf16[16,40,6144]{2,1,0:T(8,128)(2,1)S(1)} all-to-all(bf16[16,40,6144]{2,1,0:T(8,128)(2,1)S(1)} %bitcast.37), channel_id=1, replica_groups=mesh['expert'=16,'tensor'=32] {'expert'}, dimensions={0} | all-to-all | bytes 15728640 | tf_op jit(solution)/shard_map/all_to_all | solution.py:49
  190.5 2.5 fusion.2
  193.0 2.5 fusion
  195.5 2.1 stack.2
  197.6 9.3 %all-to-all-start.1 = ((bf16[32,640,84]{1,2,0:T(8,128)(2,1)}), bf16[32,640,84]{1,2,0:T(8,128)(2,1)}, u32[]{:S(2)}, u32[]{:S(2)}) async-start(bf16[32,640,84]{1,2,0:T(8,128)(2,1)} %stack.2), calls=%async_computation.1 | async-start | bytes 7208960 | tf_op jit(solution)/shard_map/all_to_all | solution.py:9
  206.9 95.4 %all-to-all-done.1 = bf16[32,640,84]{1,2,0:T(8,128)(2,1)} async-done(((bf16[32,640,84]{1,2,0:T(8,128)(2,1)}), bf16[32,640,84]{1,2,0:T(8,128)(2,1)}, u32[]{:S(2)}, u32[]{:S(2)}) %all-to-all-start.1) | async-done | bytes 3440672 | tf_op jit(solution)/shard_map/all_to_all | solution.py:9
  302.3 5.6 %reshape.123 = bf16[640,2688]{0,1:T(8,128)(2,1)} reshape(bf16[640,32,84]{0,2,1:T(8,128)(2,1)} %bitcast.6) | data formatting | bytes 6881280 | tf_op jit(solution)/shard_map/reshape | solution.py:8
  307.9 3.0 convolution_convert_fusion
  310.9 0.9 copy.19
  311.8 3.7 %all-to-all-start.2 = ((bf16[16,40,192]{2,1,0:T(8,128)(2,1)}), bf16[16,40,192]{2,1,0:T(8,128)(2,1)S(1)}, u32[]{:S(2)}, u32[]{:S(2)}) async-start(bf16[16,40,192]{2,1,0:T(8,128)(2,1)} %bitcast.8), calls=%async_computation.2 | async-start | bytes 655360 | tf_op jit(solution)/shard_map/all_to_all | solution.py:56
  315.4 0.1 fusion.8
  315.5 0.1 compare_and_fusion.1
  315.6 13.6 %all-to-all-done.2 = bf16[16,40,192]{2,1,0:T(8,128)(2,1)S(1)} async-done(((bf16[16,40,192]{2,1,0:T(8,128)(2,1)}), bf16[16,40,192]{2,1,0:T(8,128)(2,1)S(1)}, u32[]{:S(2)}, u32[]{:S(2)}) %all-to-all-start.2) | async-done | bytes 245792 | tf_op jit(solution)/shard_map/all_to_all | solution.py:56
  329.3 1.6 gather_fusion.1
  330.9 0.2 multiply_reduce_fusion
  331.1 0.7 copy.20
  (21 shorter events, 0.1 us)
Async XLA Ops:
  0.0 1.6 copy-start
  4.6 185.9 %copy-start.1 = (bf16[1,84,6144]{2,1,0:T(8,128)(2,1)S(1)}, bf16[1,84,6144]{2,1,0:T(8,128)(2,1)}, u32[]{:S(2)}) copy-start(bf16[1,84,6144]{2,1,0:T(8,128)(2,1)} %param.9) | copy-start | bytes 3096580
  190.5 2.5 copy-start.4
  197.6 104.7 %all-to-all-start.1 = ((bf16[32,640,84]{1,2,0:T(8,128)(2,1)}), bf16[32,640,84]{1,2,0:T(8,128)(2,1)}, u32[]{:S(2)}, u32[]{:S(2)}) async-start(bf16[32,640,84]{1,2,0:T(8,128)(2,1)} %stack.2), calls=%async_computation.1 | async-start | bytes 7208960 | tf_op jit(solution)/shard_map/all_to_all | solution.py:9
  302.3 5.6 %copy-start.5 = (bf16[1,192,2688]{2,1,0:T(8,128)(2,1)S(1)}, bf16[1,192,2688]{2,1,0:T(8,128)(2,1)}, u32[]{:S(2)}) copy-start(bf16[1,192,2688]{2,1,0:T(8,128)(2,1)} %param.11) | copy-start | bytes 3096580
  307.9 7.6 %copy-start.2 = (s32[128,4]{0,1:T(4,128)S(1)}, s32[128,4]{0,1:T(4,128)}, u32[]{:S(2)}) copy-start(s32[128,4]{0,1:T(4,128)} %param.7) | copy-start | bytes 6148
  307.9 7.6 %copy-start.3 = (f32[128,4]{0,1:T(4,128)S(1)}, f32[128,4]{0,1:T(4,128)}, u32[]{:S(2)}) copy-start(f32[128,4]{0,1:T(4,128)} %param.8) | copy-start | bytes 6148
  311.8 17.5 %all-to-all-start.2 = ((bf16[16,40,192]{2,1,0:T(8,128)(2,1)}), bf16[16,40,192]{2,1,0:T(8,128)(2,1)S(1)}, u32[]{:S(2)}, u32[]{:S(2)}) async-start(bf16[16,40,192]{2,1,0:T(8,128)(2,1)} %bitcast.8), calls=%async_computation.2 | async-start | bytes 655360 | tf_op jit(solution)/shard_map/all_to_all | solution.py:56
